TPU v7x, 32 devices: a whole 2x2x4 slice. The times are simulated.
32 devices in a mesh: occ: 16 (over z, y, core), vir: 2 (over x).
Axes of the slice: x: 2, y: 2, z: 4, core: 2. Of those that a mesh axis runs over, the one named last changes fastest.
Arguments:
- lambda_triples: bfloat16 [256, 320, 320], P('occ', 'vir'), may hold values from -6 to 6
- amplitude_triples: bfloat16 [256, 320, 320], P('occ', 'vir'), may hold values from -6 to 6
- spin_extent: int32 [256], P('occ'), may hold values from 80 to 320
- ladder_weight: bfloat16 [320, 320], P(None, 'vir'), may hold values from -0.3125 to 0.3125
- cycle_weight: bfloat16 [320, 40], replicated, may hold values from -0.3125 to 0.3125
- lambda_doubles: bfloat16 [40, 320], P(None, 'vir'), may hold values from -1 to 1
Outputs:
- residual: bfloat16 [256, 320, 320], P('occ', 'vir')
All inputs are finite; a program needn't handle non-finite values.
Results may differ from a plain program's by a relative error of at most 0.0043.
Values may be sent and summed in bfloat16 or wider, within the bound.
No kernel may reach another device: no remote copies, remote signals or barrier semaphores. Data moves between devices by JAX's collectives and lax.ppermute only.
A program may use at most 64 MiB of HBM per device.

v0:
```python
import jax
import jax.numpy as jnp
from jax import lax
from jax.sharding import PartitionSpec as P


def on_device(
    lambda_triples, amplitude_triples, spin_extent, ladder_weight, cycle_weight, lambda_doubles
):
    f32 = jnp.float32
    width = lambda_triples.shape[2]
    triples_all = lambda_triples.shape[0] * lax.axis_size("occ")
    columns = jnp.arange(width, dtype=jnp.int32)
    keep = columns[None, :] < spin_extent[:, None]
    masked = jnp.where(keep[:, None, :], lambda_triples, jnp.zeros_like(lambda_triples))
    ladder_full, doubles_full = (
        lax.all_gather(ladder_weight, "vir", axis=1, tiled=True),
        lax.all_gather(lambda_doubles, "vir", axis=1, tiled=True),
    )
    ladder_term = jnp.einsum("tae,eb->tab", masked, ladder_full, preferred_element_type=f32)
    cycle_mid = jnp.einsum(
        "tae,em->tam", amplitude_triples, cycle_weight, preferred_element_type=f32
    ).astype(jnp.bfloat16)
    cycle_term = jnp.einsum("tam,mb->tab", cycle_mid, doubles_full, preferred_element_type=f32)
    partial_density = jnp.einsum(
        "tae,tbe->ab",
        masked,
        lax.all_gather(amplitude_triples, "vir", axis=1, tiled=True),
        preferred_element_type=f32,
    )
    density = lax.psum(partial_density, "occ")
    density = (density / jnp.sqrt(f32(triples_all * width))).astype(jnp.bfloat16)
    density_term = jnp.einsum(
        "ac,tcb->tab",
        density,
        lax.all_gather(masked, "vir", axis=1, tiled=True),
        preferred_element_type=f32,
    )
    density_term = density_term / jnp.sqrt(f32(width))
    return (ladder_term + cycle_term + density_term).astype(jnp.bfloat16)


def solution(mesh):
    return jax.shard_map(
        on_device,
        mesh=mesh,
        in_specs=(
            P("occ", "vir", None),
            P("occ", "vir", None),
            P("occ"),
            P(None, "vir"),
            P(),
            P(None, "vir"),
        ),
        out_specs=P("occ", "vir", None),
        check_vma=False,
    )
```

profile of v0, /device:TPU:8, one launch (start us, length us, event | category | flops | bytes accessed | tf_op | source)
XLA Modules:
  0.0 227.4 jit_solution(11360172198900712387)
XLA Ops:
  6.5 0.0 copy-start
  6.5 0.0 copy-start.3
  6.5 0.0 all-gather.6.cloned.1.call-start
  6.5 0.7 all-gather.6.cloned.1.call-update
  7.3 0.0 all-gather.4.cloned.1.call-start
  7.3 0.7 iota_compare_fusion
  8.0 3.0 %broadcast_select_fusion = bf16[16,160,320]{2,1,0:T(8,128)(2,1)} fusion(bf16[16,160,320]{2,1,0:T(8,128)(2,1)} %param.6, pred[16,320]{1,0:T(8,128)(4,1)S(1)} %iota_compare_fusion), kind=kLoop, calls=%fused_computation.2 | loop fusion | flops 819200 | bytes 3281920 | tf_op jit(solution)/shard_map/jit(_where)/select_n | solution.py:15
  11.1 0.0 all-gather.4.cloned.1.call-update
  11.1 0.0 all-reduce.2.cloned.1.call-start
  11.2 0.0 copy-done.3
  11.2 4.6 %all-gather = bf16[2,160,40]{1,2,0:T(8,128)(2,1)S(1)} all-gather(bf16[1,160,40]{1,2,0:T(8,128)(2,1)S(1)} %bitcast.27), channel_id=1, replica_groups=mesh['occ'=16,'vir'=2] {'vir'}, dimensions={0}, use_global_device_ids=true | all-gather | bytes 38400 | tf_op jit(solution)/shard_map/all_gather | solution.py:18
  15.8 0.1 reshape.21
  15.9 0.0 copy-done.2
  15.9 6.4 %all_gather.12 = bf16[320,320]{0,1:T(8,128)(2,1)S(1)} all-gather(bf16[320,160]{0,1:T(8,128)(2,1)S(1)} %copy-done.2), channel_id=1, replica_groups=mesh['occ'=16,'vir'=2] {'vir'}, dimensions={1}, use_global_device_ids=true | all-gather | bytes 307200 | tf_op jit(solution)/shard_map/all_gather | solution.py:17
  22.3 4.9 %fusion.2 = f32[16,160,320]{2,1,0:T(8,128)} fusion(bf16[16,160,320]{2,1,0:T(8,128)(2,1)} %broadcast_select_fusion, bf16[320,320]{0,1:T(8,128)(2,1)S(1)} %all_gather.12), kind=kOutput, calls=%fused_computation.6 | convolution fusion | flops 524288000 | bytes 5120000 | tf_op jit(solution)/shard_map/tae,eb->tab/dot_general | solution.py:20
  27.2 36.7 %all-gather.6.cloned.1.call-done = bf16[16,320,320]{2,1,0:T(8,128)(2,1)} async-done(((bf16[16,160,320]{2,1,0:T(8,128)(2,1)}), bf16[16,320,320]{2,1,0:T(8,128)(2,1)}) %all-gather.6.cloned.1.call-update) | async-done | bytes 3276816 | tf_op jit(solution)/shard_map/all_gather | solution.py:28
  63.9 0.0 copy-done.1
  63.9 4.4 %convolution_bitcast_fusion = f32[160,320]{1,0:T(8,128)} fusion(bf16[16,160,320]{2,1,0:T(8,128)(2,1)S(1)} %copy-done.1, bf16[16,320,320]{2,1,0:T(8,128)(2,1)} %all-gather.6.cloned.1.call-done), kind=kOutput, calls=%fused_computation.5 | convolution fusion | flops 524288000 | bytes 5120000 | tf_op jit(solution)/shard_map/tae,tbe->ab/dot_general | solution.py:25
  68.3 0.0 all-reduce.2.cloned.1.call-update
  68.3 0.0 copy-done
  68.3 5.2 %fusion.1 = f32[16,160,320]{2,1,0:T(8,128)} fusion(bf16[320,40,1]{0,1,2:T(8,128)(2,1)S(1)} %reshape.21, bf16[16,160,320]{2,1,0:T(8,128)(2,1)} %param.7, bf16[320,40]{0,1:T(8,128)(2,1)S(1)} %copy-done), kind=kOutput, calls=%fused_computation.4 | convolution fusion | flops 131174400 | bytes 4966400 | tf_op jit(solution)/shard_map/tam,mb->tab/dot_general | solution.py:24
  73.5 46.9 %all-gather.4.cloned.1.call-done = bf16[16,320,320]{2,1,0:T(8,128)(2,1)} async-done(((bf16[16,160,320]{2,1,0:T(8,128)(2,1)}), bf16[16,320,320]{2,1,0:T(8,128)(2,1)}) %all-gather.4.cloned.1.call-update) | async-done | bytes 3276816 | tf_op jit(solution)/shard_map/all_gather | solution.py:36
  120.4 93.5 %all-reduce.2.cloned.1.call-done = f32[160,320]{1,0:T(8,128)} async-done(((f32[160,320]{1,0:T(8,128)}), f32[160,320]{1,0:T(8,128)}) %all-reduce.2.cloned.1.call-update) | async-done | bytes 204816 | tf_op jit(solution)/shard_map/psum | solution.py:31
  213.9 7.0 %fusion = bf16[16,160,320]{2,1,0:T(8,128)(2,1)} fusion(f32[16,160,320]{2,1,0:T(8,128)} %fusion.2, f32[16,160,320]{2,1,0:T(8,128)} %fusion.1, bf16[16,320,320]{2,1,0:T(8,128)(2,1)} %all-gather.4.cloned.1.call-done, f32[160,320]{1,0:T(8,128)} %all-reduce.2.cloned.1.call-done), kind=kOutput, calls=%fused_computation.1 | convolution fusion | flops 527667200 | bytes 11673600 | tf_op jit(solution)/shard_map/ac,tcb->tab/dot_general | solution.py:33
  (3 shorter events, 0.0 us)
Async XLA Ops:
  6.5 61.8 %copy-start = (bf16[320,40]{0,1:T(8,128)(2,1)S(1)}, bf16[320,40]{0,1:T(8,128)(2,1)}, u32[]{:S(2)}) copy-start(bf16[320,40]{0,1:T(8,128)(2,1)} %param.10) | copy-start | bytes 76804
  6.5 4.6 %copy-start.3 = (bf16[40,160]{1,0:T(8,128)(2,1)S(1)}, bf16[40,160]{1,0:T(8,128)(2,1)}, u32[]{:S(2)}) copy-start(bf16[40,160]{1,0:T(8,128)(2,1)} %param.11) | copy-start | bytes 38404
  6.5 9.4 %copy-start.2 = (bf16[320,160]{0,1:T(8,128)(2,1)S(1)}, bf16[320,160]{0,1:T(8,128)(2,1)}, u32[]{:S(2)}) copy-start(bf16[320,160]{0,1:T(8,128)(2,1)} %param.9) | copy-start | bytes 307204
  6.5 57.4 %all-gather.6.cloned.1.call-start = ((), (), s32[]{:S(2)}) async-start(), calls=%async_computation.1 | async-start | bytes 5898240 | tf_op jit(solution)/shard_map/all_gather | solution.py:28
  7.3 113.1 %all-gather.4.cloned.1.call-start = ((), (), s32[]{:S(2)}) async-start(), calls=%async_computation | async-start | bytes 5898240 | tf_op jit(solution)/shard_map/all_gather | solution.py:36
  11.1 52.8 %copy-start.1 = (bf16[16,160,320]{2,1,0:T(8,128)(2,1)S(1)}, bf16[16,160,320]{2,1,0:T(8,128)(2,1)}, u32[]{:S(2)}) copy-start(bf16[16,160,320]{2,1,0:T(8,128)(2,1)} %broadcast_select_fusion) | copy-start | bytes 4915204
  11.1 202.8 %all-reduce.2.cloned.1.call-start = ((), (), s32[]{:S(2)}) async-start(), calls=%async_computation.2 | async-start | bytes 491520 | tf_op jit(solution)/shard_map/psum | solution.py:31
Sparse Core Ops, SparseCore 0:
  8.9 54.9 all-gather.5
  65.4 54.8 all-gather.3
  123.8 90.0 all-reduce.1
where the time goes:
time: 228 us; the launch traced here: 227 us
  waiting for transfers between devices  178 us (78%)
  matrix products  21.4 us (9%)
  between operations  13.1 us (6%)
  blocking collectives  11 us (5%)
  other arithmetic  3.77 us (2%)
    psum x1, waiting for transfers between devices, on_device(): density = lax.psum(partial_density, 'occ')  93.5 us
    all_gather x1, waiting for transfers between devices, on_device(): lax.all_gather(masked, 'vir', axis=1, tiled=True)  46.9 us
    all_gather x1, waiting for transfers between devices, on_device(): lax.all_gather(amplitude_triples, 'vir', axis=1, tiled=True)  36.7 us
    dot_general x1, matrix products, on_device(): jnp.einsum('ac,tcb->tab', density, lax.all_gather(masked, 'vir', axis=1,...  6.97 us
    all_gather x1, blocking collectives, on_device(): lax.all_gather(ladder_weight, 'vir', axis=1, tiled=True)  6.43 us
    dot_general x1, matrix products, on_device(): jnp.einsum('tam,mb->tab', cycle_mid, doubles_full, preferred_element_type...  5.16 us
    dot_general x1, matrix products, on_device(): jnp.einsum('tae,eb->tab', masked, ladder_full, preferred_element_type=f32)  4.91 us
    all_gather x1, blocking collectives, on_device(): lax.all_gather(lambda_doubles, 'vir', axis=1, tiled=True)  4.59 us
  transfers between devices with their start and end apart: 3, of which 3 were waited for; matrix products, arithmetic and copies ran while one was open for 8% of the time, Pallas kernels for 0%

commit v1 on v0

--- a/solution.py
+++ b/solution.py
@@ -28,7 +28,8 @@
         lax.all_gather(amplitude_triples, "vir", axis=1, tiled=True),
         preferred_element_type=f32,
     )
-    density = lax.psum(partial_density, "occ")
+    terms = lax.all_gather(partial_density, "occ")
+    density = jnp.sum(terms, axis=0)
     density = (density / jnp.sqrt(f32(triples_all * width))).astype(jnp.bfloat16)
     density_term = jnp.einsum(
         "ac,tcb->tab",

time: 228 us -> 187 us (0.82)
  waiting for transfers between devices: 178 us -> 137 us
    psum x1 -> x0, waiting for transfers between devices: 93.5 us -> none  [on_device(): density = lax.psum(partial_density, 'occ')]
    all_gather x0 -> x1, waiting for transfers between devices: none -> 30.1 us  [on_device(): terms = lax.all_gather(partial_density, 'occ')]
    all_gather x1, waiting for transfers between devices: 36.7 us -> 54 us  [on_device(): lax.all_gather(amplitude_triples, 'vir', axis=1, tiled=True)]
    all_gather x1, waiting for transfers between devices: 46.9 us -> 51.5 us  [on_device(): lax.all_gather(masked, 'vir', axis=1, tiled=True)]
    reduce_sum x0 -> x1, other arithmetic: none -> 2.35 us  [on_device(): density = jnp.sum(terms, axis=0)]
  transfers between devices with their start and end apart: 3 -> 3, of which waited for: 3 -> 3; matrix products, arithmetic and copies ran while one was open for 8% -> 7% of each run, Pallas kernels for 0% -> 0%
where the time goes in v1:
time: 187 us; the launch traced here: 185 us
  waiting for transfers between devices  137 us (73%)
  matrix products  19.8 us (11%)
  between operations  13.2 us (7%)
  blocking collectives  10.1 us (5%)
  other arithmetic  4.85 us (3%)
    all_gather x1, waiting for transfers between devices, on_device(): lax.all_gather(amplitude_triples, 'vir', axis=1, tiled=True)  54 us
    all_gather x1, waiting for transfers between devices, on_device(): lax.all_gather(masked, 'vir', axis=1, tiled=True)  51.5 us
    all_gather x1, waiting for transfers between devices, on_device(): terms = lax.all_gather(partial_density, 'occ')  30.1 us
    dot_general x1, matrix products, on_device(): jnp.einsum('ac,tcb->tab', density, lax.all_gather(masked, 'vir', axis=1,...  6.9 us
    all_gather x1, blocking collectives, on_device(): lax.all_gather(ladder_weight, 'vir', axis=1, tiled=True)  5.56 us
    dot_general x1, matrix products, on_device(): jnp.einsum('tam,mb->tab', cycle_mid, doubles_full, preferred_element_type...  5.13 us
    all_gather x1, blocking collectives, on_device(): lax.all_gather(lambda_doubles, 'vir', axis=1, tiled=True)  4.59 us
    dot_general x1, matrix products, on_device(): jnp.einsum('tae,tbe->ab', masked, lax.all_gather(amplitude_triples, 'vir'...  4.43 us
  transfers between devices with their start and end apart: 3, of which 3 were waited for; matrix products, arithmetic and copies ran while one was open for 7% of the time, Pallas kernels for 0%

profile of v1, /device:TPU:8, one launch (start us, length us, event | category | flops | bytes accessed | tf_op | source)
XLA Modules:
  0.0 185.2 jit_solution(13088541682213249340)
XLA Ops:
  6.5 0.0 copy-start
  6.5 0.7 all-gather.8.cloned.1.call-update
  7.3 0.0 all-gather.10.cloned.1.call-start
  7.3 0.7 iota_compare_fusion
  8.0 1.8 broadcast_select_fusion
  9.8 0.0 copy-start.1
  9.8 0.0 copy-start.4
  9.8 0.0 copy-start.3
  9.8 54.0 %all-gather.8.cloned.1.call-done = bf16[16,320,320]{2,1,0:T(8,128)(2,1)} async-done(((bf16[16,160,320]{2,1,0:T(8,128)(2,1)}), bf16[16,320,320]{2,1,0:T(8,128)(2,1)}) %all-gather.8.cloned.1.call-update) | async-done | bytes 3276816 | tf_op jit(solution)/shard_map/all_gather | solution.py:28
  63.9 4.4 %convolution_bitcast_fusion = f32[160,320]{1,0:T(8,128)} fusion(bf16[16,160,320]{2,1,0:T(8,128)(2,1)S(1)} %broadcast_select_fusion, bf16[16,320,320]{2,1,0:T(8,128)(2,1)} %all-gather.8.cloned.1.call-done), kind=kOutput, calls=%fused_computation.5 | convolution fusion | flops 524288000 | bytes 5120000 | tf_op jit(solution)/shard_map/tae,tbe->ab/dot_general | solution.py:25
  68.3 0.0 all-gather.10.cloned.1.call-update
  68.3 0.0 all-gather.6.cloned.1.call-start
  68.4 0.7 all-gather.6.cloned.1.call-update
  69.1 0.0 copy-start.2
  69.1 0.0 copy-done.4
  69.1 4.6 %all-gather.1 = bf16[2,160,40]{1,2,0:T(8,128)(2,1)S(1)} all-gather(bf16[1,160,40]{1,2,0:T(8,128)(2,1)S(1)} %bitcast.29), channel_id=1, replica_groups=mesh['occ'=16,'vir'=2] {'vir'}, dimensions={0}, use_global_device_ids=true | all-gather | bytes 38400 | tf_op jit(solution)/shard_map/all_gather | solution.py:18
  73.7 0.1 reshape.22
  73.8 5.6 %all_gather.18 = bf16[320,320]{0,1:T(8,128)(2,1)S(1)} all-gather(bf16[320,160]{0,1:T(8,128)(2,1)S(1)} %copy-done.3), channel_id=1, replica_groups=mesh['occ'=16,'vir'=2] {'vir'}, dimensions={1}, use_global_device_ids=true | all-gather | bytes 307200 | tf_op jit(solution)/shard_map/all_gather | solution.py:17
  79.4 5.1 %fusion.1 = f32[16,160,320]{2,1,0:T(8,128)} fusion(bf16[320,40,1]{0,1,2:T(8,128)(2,1)S(1)} %reshape.22, bf16[16,160,320]{2,1,0:T(8,128)(2,1)} %param.7, bf16[320,40]{0,1:T(8,128)(2,1)S(1)} %copy-done), kind=kOutput, calls=%fused_computation.4 | convolution fusion | flops 131174400 | bytes 4966400 | tf_op jit(solution)/shard_map/tam,mb->tab/dot_general | solution.py:24
  84.5 3.3 %fusion.2 = f32[16,160,320]{2,1,0:T(8,128)} fusion(bf16[16,160,320]{2,1,0:T(8,128)(2,1)S(1)} %copy-done.2, bf16[320,320]{0,1:T(8,128)(2,1)S(1)} %all_gather.18), kind=kOutput, calls=%fused_computation.6 | convolution fusion | flops 524288000 | bytes 5120000 | tf_op jit(solution)/shard_map/tae,eb->tab/dot_general | solution.py:20
  87.8 30.1 %all-gather.10.cloned.1.call-done = f32[2560,320]{1,0:T(8,128)} async-done(((f32[160,320]{1,0:T(8,128)}), f32[2560,320]{1,0:T(8,128)}) %all-gather.10.cloned.1.call-update) | async-done | bytes 3276816 | tf_op jit(solution)/shard_map/all_gather | solution.py:31
  117.9 2.4 %reduce_sum.9 = f32[160,320]{1,0:T(8,128)S(1)} reduce(f32[16,160,320]{2,1,0:T(8,128)} %bitcast.28, f32[]{:T(128)} %constant.3.clone.1), dimensions={0}, to_apply=%region_0.1 | reduce | flops 768000 | bytes 3481604 | tf_op jit(solution)/shard_map/reduce_sum | solution.py:32
  120.3 51.5 %all-gather.6.cloned.1.call-done = bf16[16,320,320]{2,1,0:T(8,128)(2,1)} async-done(((bf16[16,160,320]{2,1,0:T(8,128)(2,1)}), bf16[16,320,320]{2,1,0:T(8,128)(2,1)}) %all-gather.6.cloned.1.call-update) | async-done | bytes 3276816 | tf_op jit(solution)/shard_map/all_gather | solution.py:37
  171.8 6.9 %fusion = bf16[16,160,320]{2,1,0:T(8,128)(2,1)} fusion(f32[16,160,320]{2,1,0:T(8,128)} %fusion.2, f32[16,160,320]{2,1,0:T(8,128)} %fusion.1, bf16[16,320,320]{2,1,0:T(8,128)(2,1)} %all-gather.6.cloned.1.call-done, f32[160,320]{1,0:T(8,128)S(1)} %reduce_sum.9), kind=kOutput, calls=%fused_computation.1 | convolution fusion | flops 527667200 | bytes 11673600 | tf_op jit(solution)/shard_map/ac,tcb->tab/dot_general | solution.py:34
  (6 shorter events, 0.0 us)
Async XLA Ops:
  6.5 72.9 %copy-start = (bf16[320,40]{0,1:T(8,128)(2,1)S(1)}, bf16[320,40]{0,1:T(8,128)(2,1)}, u32[]{:S(2)}) copy-start(bf16[320,40]{0,1:T(8,128)(2,1)} %param.10) | copy-start | bytes 76804
  6.5 57.4 %all-gather.8.cloned.1.call-start = ((), (), s32[]{:S(2)}) async-start(), calls=%async_computation.1 | async-start | bytes 5898240 | tf_op jit(solution)/shard_map/all_gather | solution.py:28
  7.3 110.7 %all-gather.10.cloned.1.call-start = ((), (), s32[]{:S(2)}) async-start(), calls=%async_computation.2 | async-start | bytes 4177920 | tf_op jit(solution)/shard_map/all_gather | solution.py:31
  9.8 58.6 %copy-start.1 = (bf16[16,160,320]{2,1,0:T(8,128)(2,1)}, bf16[16,160,320]{2,1,0:T(8,128)(2,1)S(1)}, u32[]{:S(2)}) copy-start(bf16[16,160,320]{2,1,0:T(8,128)(2,1)S(1)} %broadcast_select_fusion) | copy-start | bytes 4915204
  9.8 59.3 %copy-start.4 = (bf16[40,160]{1,0:T(8,128)(2,1)S(1)}, bf16[40,160]{1,0:T(8,128)(2,1)}, u32[]{:S(2)}) copy-start(bf16[40,160]{1,0:T(8,128)(2,1)} %param.11) | copy-start | bytes 38404
  9.8 64.0 %copy-start.3 = (bf16[320,160]{0,1:T(8,128)(2,1)S(1)}, bf16[320,160]{0,1:T(8,128)(2,1)}, u32[]{:S(2)}) copy-start(bf16[320,160]{0,1:T(8,128)(2,1)} %param.9) | copy-start | bytes 307204
  68.3 103.4 %all-gather.6.cloned.1.call-start = ((), (), s32[]{:S(2)}) async-start(), calls=%async_computation | async-start | bytes 5898240 | tf_op jit(solution)/shard_map/all_gather | solution.py:37
  69.1 15.4 %copy-start.2 = (bf16[16,160,320]{2,1,0:T(8,128)(2,1)S(1)}, bf16[16,160,320]{2,1,0:T(8,128)(2,1)}, u32[]{:S(2)}) copy-start(bf16[16,160,320]{2,1,0:T(8,128)(2,1)} %copy-done.1) | copy-start | bytes 4915204
Sparse Core Ops, SparseCore 0:
  8.9 54.9 all-gather.7
  68.5 49.4 all-gather.9
  119.5 52.2 all-gather.5
